TPU v7x, 512 devices: a whole 4x8x8 slice. The times are simulated.
512 devices in a mesh: kv: 8 (over x, core), seq: 64 (over z, y).
Axes of the slice: x: 4, y: 8, z: 8, core: 2. Of those that a mesh axis runs over, the one named last changes fastest.
Arguments:
- queries: bfloat16 [512, 4096], P(('kv', 'seq')), may hold values from -6 to 6
- out_grad: bfloat16 [512, 4096], P(('kv', 'seq')), may hold values from -3072 to 3072
- saved_out: bfloat16 [512, 4096], P(('kv', 'seq')), may hold values from -1.5 to 1.5
- saved_lse: float32 [512, 32], P(('kv', 'seq')), as said below
- video_keys: bfloat16 [16384, 1024], P('seq', 'kv'), may hold values from -6 to 6
- video_values: bfloat16 [16384, 1024], P('seq', 'kv'), may hold values from -6 to 6
Outputs:
- grad_queries: bfloat16 [512, 4096], P(('kv', 'seq'))
- grad_keys: bfloat16 [16384, 1024], P('seq', 'kv')
- grad_values: bfloat16 [16384, 1024], P('seq', 'kv')
Inputs may be any that keep to these rules, and one draw needn't show every extreme that they name: saved_lse lies between log(16384) and log(16384) + 1.5.
All inputs are finite; a program needn't handle non-finite values.
Results may differ from a plain program's by a relative error of at most 0.0057.
Values may be sent and summed in bfloat16 or wider, within the bound.
A program may use at most 64 MiB of HBM per device.

v0:
```python
import math
import jax
import jax.numpy as jnp
from jax import lax
from jax.sharding import PartitionSpec as P


def head_columns(block, first, width):
    return lax.dynamic_slice_in_dim(block, first, width, 1)


def seq_major(block, kv_count, seq_count):
    total_rows = block.shape[0]
    width = block.shape[1]
    shaped = block.reshape(kv_count, seq_count, total_rows // (kv_count * seq_count), width)
    return shaped.transpose(1, 0, 2, 3).reshape(total_rows, width)


def make_accumulate(
    lse_group,
    delta_group,
    group_index,
    group_width,
    group_heads,
    head_width,
    score_scale,
    video_keys,
    video_values,
):

    def accumulate(totals, pieces, offset):
        key_total, value_total, query_rows = totals
        query_block, grad_block = pieces
        query_block = head_columns(query_block, group_index * group_width, group_width)
        grad_block = head_columns(grad_block, group_index * group_width, group_width)
        columns = []
        for member in range(group_heads):
            query_head = query_block[:, member * head_width : (member + 1) * head_width]
            grad_head = grad_block[:, member * head_width : (member + 1) * head_width]
            scores = (
                jnp.einsum("nd,kd->nk", query_head, video_keys, preferred_element_type=jnp.float32)
                * score_scale
            )
            probs = jnp.exp(scores - lse_group[:, member : member + 1])
            probs_half = probs.astype(jnp.bfloat16)
            value_total = value_total + jnp.einsum(
                "nk,nd->kd", probs_half, grad_head, preferred_element_type=jnp.float32
            )
            dprobs = jnp.einsum(
                "nd,kd->nk", grad_head, video_values, preferred_element_type=jnp.float32
            )
            dscores = (probs * (dprobs - delta_group[:, member : member + 1])).astype(jnp.bfloat16)
            key_total = key_total + jnp.einsum(
                "nk,nd->kd", dscores, query_head, preferred_element_type=jnp.float32
            )
            columns.append(
                jnp.einsum("nk,kd->nd", dscores, video_keys, preferred_element_type=jnp.float32)
            )
        query_rows = jnp.concatenate(columns, axis=1)
        return (key_total, value_total, query_rows)

    return accumulate


def shards(queries, out_grad, saved_out, saved_lse, video_keys, video_values):
    kv_count = lax.axis_size("kv")
    seq_count = lax.axis_size("seq")
    group_index = lax.axis_index("kv")
    head_width = video_keys.shape[1]
    group_heads = saved_lse.shape[1] // kv_count
    group_width = group_heads * head_width
    own_rows = queries.shape[0]
    total_rows = own_rows * kv_count * seq_count
    score_scale = 1.0 / math.sqrt(head_width)
    products = out_grad.astype(jnp.float32) * saved_out.astype(jnp.float32)
    own_delta = products.reshape(own_rows, -1, head_width).sum(axis=2)
    lse_all, delta_all = (
        lax.all_gather(saved_lse, ("kv", "seq"), axis=0, tiled=True),
        lax.all_gather(own_delta, ("kv", "seq"), axis=0, tiled=True),
    )
    lse_wide = head_columns(lse_all, group_index * group_heads, group_heads)
    delta_wide = head_columns(delta_all, group_index * group_heads, group_heads)
    key_rows = video_keys.shape[0]
    initial = (
        jnp.zeros((key_rows, head_width), jnp.float32),
        jnp.zeros((key_rows, head_width), jnp.float32),
        jnp.zeros((total_rows, group_width), jnp.float32),
    )
    wide_step = make_accumulate(
        lse_wide,
        delta_wide,
        group_index,
        group_width,
        group_heads,
        head_width,
        score_scale,
        video_keys,
        video_values,
    )
    gathered = (
        lax.all_gather(queries, ("kv", "seq"), axis=0, tiled=True),
        lax.all_gather(out_grad, ("kv", "seq"), axis=0, tiled=True),
    )
    key_total, value_total, query_rows = wide_step(initial, gathered, 0)
    query_rows = seq_major(query_rows, kv_count, seq_count)
    summed = lax.psum_scatter(
        query_rows.reshape(seq_count, total_rows // seq_count, group_width),
        "seq",
        scatter_dimension=0,
        tiled=True,
    )
    rounded = (summed * score_scale).astype(jnp.bfloat16).reshape(kv_count, own_rows, group_width)
    returned = lax.all_to_all(rounded, "kv", split_axis=0, concat_axis=2, tiled=True)
    grad_queries = returned.reshape(own_rows, kv_count * group_width)
    return (
        grad_queries,
        (key_total * score_scale).astype(jnp.bfloat16),
        value_total.astype(jnp.bfloat16),
    )


def solution(mesh):
    return jax.shard_map(
        shards,
        mesh=mesh,
        in_specs=(
            P(("kv", "seq"), None),
            P(("kv", "seq"), None),
            P(("kv", "seq"), None),
            P(("kv", "seq"), None),
            P("seq", "kv"),
            P("seq", "kv"),
        ),
        out_specs=(P(("kv", "seq"), None), P("seq", "kv"), P("seq", "kv")),
        check_vma=False,
    )
```

profile of v0, /device:TPU:1, one launch (start us, length us, event | category | flops | bytes accessed | tf_op | source)
XLA Modules:
  0.0 824.8 jit_solution(11572126414588842598)
XLA Ops:
  7.2 0.0 copy-start
  7.2 0.0 copy-start.4
  7.2 0.0 all-reduce.5.cloned.1.call-start
  7.2 0.8 convert_multiply_fusion
  8.0 0.1 reduce_sum.11
  8.1 0.3 dynamic-update-slice
  8.4 0.8 reshape.27
  9.2 0.0 all-reduce.5.cloned.1.call-update
  9.3 0.0 all-gather.7.cloned.1.call-start
  9.3 0.7 all-gather.7.cloned.1.call-update
  10.0 0.0 all-gather.9.cloned.1.call-start
  10.1 0.7 all-gather.9.cloned.1.call-update
  10.7 0.0 reduce-scatter.4.cloned.1.call-start
  10.8 66.6 %all-gather.2 = f32[512,1,32]{2,1,0:T(1,128)S(1)} all-gather(f32[1,1,32]{2,1,0:T(1,128)} %bitcast.70), channel_id=1, replica_groups=mesh['kv'=8,'seq'=64] {'kv','seq'}, dimensions={0}, use_global_device_ids=true | all-gather | bytes 65664 | tf_op jit(solution)/shard_map/all_gather | solution.py:78
  77.4 0.6 constant_dynamic-slice_fusion.1
  78.0 0.1 copy.14
  78.1 212.3 %all-reduce.5.cloned.1.call-done = f32[512,32]{1,0:T(8,128)} async-done(((f32[512,32]{1,0:T(8,128)}), f32[512,32]{1,0:T(8,128)}) %all-reduce.5.cloned.1.call-update) | async-done | bytes 65552
  290.5 2.0 dynamic-slice_reduce_fusion.3
  292.5 127.6 %all-gather.7.cloned.1.call-done = bf16[512,1,4096]{2,1,0:T(2,128)(2,1)} async-done(((bf16[1,1,4096]{2,1,0:T(2,128)(2,1)}), bf16[512,1,4096]{2,1,0:T(2,128)(2,1)}) %all-gather.7.cloned.1.call-update) | async-done | bytes 4194320 | tf_op jit(solution)/shard_map/all_gather | solution.py:101
  420.0 2.3 constant_dynamic-slice_fusion.2
  422.3 0.1 copy.24
  422.5 126.2 %all-gather.9.cloned.1.call-done = bf16[512,1,4096]{2,1,0:T(2,128)(2,1)} async-done(((bf16[1,1,4096]{2,1,0:T(2,128)(2,1)}), bf16[512,1,4096]{2,1,0:T(2,128)(2,1)}) %all-gather.9.cloned.1.call-update) | async-done | bytes 4194320 | tf_op jit(solution)/shard_map/all_gather | solution.py:102
  548.7 2.3 constant_dynamic-slice_fusion
  551.0 0.1 copy.23
  551.1 0.0 copy-done
  551.1 0.2 fusion.10
  551.4 0.0 copy-done.4
  551.4 0.2 fusion.12
  551.6 0.2 fusion.46
  551.8 0.2 fusion.7
  552.1 0.2 fusion.13
  552.3 0.0 copy-start.1
  552.3 0.2 fusion.45
  552.6 0.2 fusion.4
  552.8 0.2 fusion.14
  553.1 0.0 copy-start.2
  553.1 0.2 fusion.44
  553.3 0.0 copy-done.1
  553.3 0.4 copy-done.2
  553.8 0.2 fusion.1
  554.0 0.2 fusion.15
  554.3 0.0 copy-start.3
  554.3 0.7 copy-done.3
  555.0 0.2 fusion.43
  555.2 1.1 pad_maximum_fusion
  556.3 2.6 copy.16
  558.9 2.8 copy.17
  561.7 0.0 reduce-scatter.4.cloned.1.call-update
  561.7 1.2 fusion.38
  562.9 1.2 convolution_add_fusion.5
  564.2 1.9 convolution_add_fusion.4
  566.0 0.3 fusion.22
  566.3 0.3 convolution_add_fusion.2
  566.6 0.3 convolution_add_fusion.1
  566.8 0.9 fusion.18
  567.7 233.1 %reduce-scatter.4.cloned.1.call-done = f32[1,8,512]{2,1,0:T(8,128)} async-done(((f32[64,8,512]{2,1,0:T(8,128)}), f32[1,8,512]{2,1,0:T(8,128)}) %reduce-scatter.4.cloned.1.call-update) | async-done | bytes 16400
  800.9 0.7 fusion.41
  801.6 0.5 broadcast.13
  802.1 0.6 reduce.9
  802.8 0.6 reshape.44
  803.4 9.7 %all-to-all-start = ((bf16[8,2,256]{2,1,0:T(2,128)(2,1)}), bf16[8,2,256]{2,1,0:T(2,128)(2,1)S(1)}, u32[]{:S(2)}, u32[]{:S(2)}) async-start(bf16[8,2,256]{2,1,0:T(2,128)(2,1)} %reshape.44), calls=%async_computation | async-start | bytes 16384 | tf_op jit(solution)/shard_map/all_to_all | solution.py:113
  813.0 1.8 fusion.17
  814.9 2.8 all-to-all-done
  817.7 0.6 reshape.45
  (2 shorter events, 0.0 us)
Async XLA Ops:
  7.2 543.9 %copy-start = (bf16[256,128]{1,0:T(8,128)(2,1)S(1)}, bf16[256,128]{1,0:T(8,128)(2,1)}, u32[]{:S(2)}) copy-start(bf16[256,128]{1,0:T(8,128)(2,1)} %param.10) | copy-start | bytes 196612
  7.2 544.2 %copy-start.4 = (bf16[256,128]{1,0:T(8,128)(2,1)S(1)}, bf16[256,128]{1,0:T(8,128)(2,1)}, u32[]{:S(2)}) copy-start(bf16[256,128]{1,0:T(8,128)(2,1)} %param.11) | copy-start | bytes 196612
  7.2 283.3 %all-reduce.5.cloned.1.call-start = ((), (), s32[]{:S(2)}) async-start(), calls=%async_computation.4 | async-start | bytes 524288
  9.3 410.8 %all-gather.7.cloned.1.call-start = ((), (), s32[]{:S(2)}) async-start(), calls=%async_computation.2 | async-start | bytes 8404992 | tf_op jit(solution)/shard_map/all_gather | solution.py:101
  10.0 538.6 %all-gather.9.cloned.1.call-start = ((), (), s32[]{:S(2)}) async-start(), calls=%async_computation.3 | async-start | bytes 8404992 | tf_op jit(solution)/shard_map/all_gather | solution.py:102
  10.7 790.1 %reduce-scatter.4.cloned.1.call-start = ((), (), s32[]{:S(2)}) async-start(), calls=%async_computation.5 | async-start | bytes 1064960
  552.3 1.0 copy-start.1
  553.1 0.7 copy-start.2
  554.3 0.7 copy-start.3
  803.4 14.3 %all-to-all-start = ((bf16[8,2,256]{2,1,0:T(2,128)(2,1)}), bf16[8,2,256]{2,1,0:T(2,128)(2,1)S(1)}, u32[]{:S(2)}, u32[]{:S(2)}) async-start(bf16[8,2,256]{2,1,0:T(2,128)(2,1)} %reshape.44), calls=%async_computation | async-start | bytes 16384 | tf_op jit(solution)/shard_map/all_to_all | solution.py:113
Sparse Core Ops, SparseCore 0:
  13.0 277.4 all-reduce.4
  294.9 125.1 all-gather.6
  424.5 124.1 all-gather.8
  561.8 239.0 reduce-scatter.3
where the time goes:
time: 825 us
  waiting for transfers between devices  703 us (85%)
  blocking collectives  66.6 us (8%)
  local copies, waits for them, and re-layouts  17 us (2%)
  between operations  14 us (2%)
  matrix products  10.7 us (1%)
  starting transfers between devices  9.82 us (1%)
    unnamed x6, waiting for transfers between devices  447 us
    all_gather x1, waiting for transfers between devices, shards(): lax.all_gather(queries, ('kv', 'seq'), axis=0, tiled=True)  128 us
    all_gather x1, waiting for transfers between devices, shards(): lax.all_gather(out_grad, ('kv', 'seq'), axis=0, tiled=True)  126 us
    all_gather x1, blocking collectives, shards(): lax.all_gather(saved_lse, ('kv', 'seq'), axis=0, tiled=True)  66.6 us
  transfers between devices with their start and end apart: 5, of which 5 were waited for; matrix products, arithmetic and copies ran while one was open for 2% of the time, Pallas kernels for 0%

commit v1 on v0

--- a/solution.py
+++ b/solution.py
@@ -98,7 +98,15 @@
         video_values,
     )
     gathered = (
-        lax.all_gather(queries, ("kv", "seq"), axis=0, tiled=True),
+        jnp.concatenate(
+            lax.all_to_all(
+                jnp.stack([queries for _ in range(lax.axis_size(("kv", "seq")))]),
+                ("kv", "seq"),
+                0,
+                0,
+            ),
+            axis=0,
+        ),
         lax.all_gather(out_grad, ("kv", "seq"), axis=0, tiled=True),
     )
     key_total, value_total, query_rows = wide_step(initial, gathered, 0)

time: 825 us -> 779 us (0.944)
  waiting for transfers between devices: 703 us -> 487 us
  blocking collectives: 66.6 us -> 144 us
  local copies, waits for them, and re-layouts: 17 us -> 56.1 us
  other arithmetic: 3.31 us -> 31.5 us
  starting transfers between devices: 9.82 us -> 34.1 us
    all_gather x1 -> x0, waiting for transfers between devices: 128 us -> none  [shards(): lax.all_gather(queries, ('kv', 'seq'), axis=0, tiled=True)]
    unnamed x6 -> x5, waiting for transfers between devices: 447 us -> 357 us
    all_gather x1, blocking collectives: 66.6 us -> 144 us  [shards(): lax.all_gather(saved_lse, ('kv', 'seq'), axis=0, tiled=True)]
    unnamed x16 -> x20, local copies, waits for them, and re-layouts: 2.92 us -> 36.5 us
    another operation x0 -> x1, other arithmetic: none -> 27.4 us  [shards(): jnp.stack([queries for _ in range(lax.axis_size(('kv', 'seq')))])]
    all_to_all x0 -> x1, starting transfers between devices: none -> 24.2 us  [shards(): lax.all_to_all(jnp.stack([queries for _ in range(lax.axis_size(('kv', 'se...]
  transfers between devices with their start and end apart: 5 -> 5, of which waited for: 5 -> 4; matrix products, arithmetic and copies ran while one was open for 2% -> 7% of each run, Pallas kernels for 0% -> 0%
where the time goes in v1:
time: 779 us; the launch traced here: 777 us
  waiting for transfers between devices  487 us (63%)
  blocking collectives  144 us (18%)
  local copies, waits for them, and re-layouts  56.1 us (7%)
  starting transfers between devices  34.1 us (4%)
  other arithmetic  31.5 us (4%)
  between operations  14 us (2%)
  matrix products  10.6 us (1%)
    unnamed x5, waiting for transfers between devices  357 us
    all_gather x1, blocking collectives, shards(): lax.all_gather(saved_lse, ('kv', 'seq'), axis=0, tiled=True)  144 us
    all_gather x1, waiting for transfers between devices, shards(): lax.all_gather(out_grad, ('kv', 'seq'), axis=0, tiled=True)  128 us
    unnamed x20, local copies, waits for them, and re-layouts  36.5 us
    another operation x1, other arithmetic, shards(): jnp.stack([queries for _ in range(lax.axis_size(('kv', 'seq')))])  27.4 us
    all_to_all x1, starting transfers between devices, shards(): lax.all_to_all(jnp.stack([queries for _ in range(lax.axis_size(('kv', 'se...  24.2 us
  transfers between devices with their start and end apart: 5, of which 4 were waited for; matrix products, arithmetic and copies ran while one was open for 7% of the time, Pallas kernels for 0%

profile of v1, /device:TPU:1, one launch (start us, length us, event | category | flops | bytes accessed | tf_op | source)
XLA Modules:
  0.0 777.1 jit_solution(12828912137582704239)
XLA Ops:
  7.2 0.0 copy-start
  7.2 0.0 all-reduce.5.cloned.1.call-start
  7.2 0.8 convert_multiply_fusion
  8.0 0.1 reduce_sum.11
  8.1 0.3 dynamic-update-slice
  8.4 0.8 reshape.32
  9.2 0.0 all-reduce.5.cloned.1.call-update
  9.2 0.0 all-gather.5.cloned.1.call-start
  9.3 0.7 all-gather.5.cloned.1.call-update
  10.0 0.8 reduce.1
  10.8 5.6 stack.2
  16.4 0.5 broadcast.17
  16.9 27.4 %reduce.10 = bf16[512,4096]{1,0:T(8,128)(2,1)} reduce(bf16[512,1,4096]{2,1,0:T(2,128)(2,1)} %stack.2, bf16[]{:T(256)} %broadcast.17), dimensions={1}, to_apply=%stack.2.reduce_sub_computation | reduce | bytes 8388610 | tf_op jit(solution)/shard_map/stack | solution.py:103
  44.3 7.9 %reshape.47 = bf16[512,2,2048]{2,1,0:T(2,128)(2,1)} reshape(bf16[512,4096]{1,0:T(8,128)(2,1)} %reduce.10) | data formatting | bytes 8388608
  52.1 24.2 %all-to-all-start = ((bf16[512,2,2048]{2,1,0:T(2,128)(2,1)}), bf16[512,2,2048]{2,1,0:T(2,128)(2,1)}, u32[]{:S(2)}, u32[]{:S(2)}) async-start(bf16[512,2,2048]{2,1,0:T(2,128)(2,1)} %reshape.47), calls=%async_computation | async-start | bytes 8388608 | tf_op jit(solution)/shard_map/all_to_all | solution.py:102
  76.4 0.0 reduce-scatter.4.cloned.1.call-start
  76.4 0.0 copy-done.5
  76.4 143.6 %all-gather.1 = f32[512,1,32]{2,1,0:T(1,128)S(1)} all-gather(f32[1,1,32]{2,1,0:T(1,128)S(1)} %bitcast.68), channel_id=1, replica_groups=mesh['kv'=8,'seq'=64] {'kv','seq'}, dimensions={0}, use_global_device_ids=true | all-gather | bytes 65664 | tf_op jit(solution)/shard_map/all_gather | solution.py:78
  220.1 0.6 constant_dynamic-slice_fusion.1
  220.7 0.1 copy.14
  220.8 122.8 %all-reduce.5.cloned.1.call-done = f32[512,32]{1,0:T(8,128)} async-done(((f32[512,32]{1,0:T(8,128)}), f32[512,32]{1,0:T(8,128)}) %all-reduce.5.cloned.1.call-update) | async-done | bytes 65552
  343.6 1.9 dynamic-slice_reduce_fusion.3
  345.6 127.6 %all-gather.5.cloned.1.call-done = bf16[512,1,4096]{2,1,0:T(2,128)(2,1)} async-done(((bf16[1,1,4096]{2,1,0:T(2,128)(2,1)}), bf16[512,1,4096]{2,1,0:T(2,128)(2,1)}) %all-gather.5.cloned.1.call-update) | async-done | bytes 4194320 | tf_op jit(solution)/shard_map/all_gather | solution.py:110
  473.2 2.3 constant_dynamic-slice_fusion
  475.5 0.1 copy.23
  475.7 0.0 copy-start.4
  475.7 0.0 all-to-all-done
  475.7 26.6 %reshape.48 = bf16[512,1,4096]{2,1,0:T(2,128)(2,1)} reshape(bf16[512,2,2048]{2,1,0:T(2,128)(2,1)} %all-to-all-done) | data formatting | bytes 8388608
  502.3 2.3 constant_dynamic-slice_fusion.2
  504.6 0.1 copy.24
  504.7 0.0 copy-done
  504.7 0.2 fusion.1
  505.0 0.2 fusion.4
  505.2 0.2 fusion.7
  505.5 0.2 fusion.10
  505.7 0.0 copy-done.4
  505.7 0.2 fusion.15
  506.0 0.2 fusion.43
  506.2 0.2 fusion.14
  506.5 0.2 fusion.44
  506.7 0.2 fusion.13
  507.0 0.2 fusion.45
  507.2 0.2 fusion.12
  507.5 0.2 copy-done.3
  507.7 0.2 fusion.46
  507.9 1.1 pad_maximum_fusion
  509.0 2.6 copy.16
  511.6 2.8 copy.17
  514.4 0.0 reduce-scatter.4.cloned.1.call-update
  514.4 1.2 fusion.38
  515.6 1.2 convolution_add_fusion.5
  516.9 1.9 convolution_add_fusion.4
  518.7 0.3 fusion.22
  519.0 0.3 convolution_add_fusion.2
  519.3 0.3 convolution_add_fusion.1
  519.5 0.9 fusion.18
  520.4 233.1 %reduce-scatter.4.cloned.1.call-done = f32[1,8,512]{2,1,0:T(8,128)} async-done(((f32[64,8,512]{2,1,0:T(8,128)}), f32[1,8,512]{2,1,0:T(8,128)}) %reduce-scatter.4.cloned.1.call-update) | async-done | bytes 16400
  753.5 0.7 fusion.41
  754.3 0.6 reduce.11
  754.9 0.6 reshape.49
  755.5 9.8 %all-to-all-start.1 = ((bf16[8,2,256]{2,1,0:T(2,128)(2,1)}), bf16[8,2,256]{2,1,0:T(2,128)(2,1)S(1)}, u32[]{:S(2)}, u32[]{:S(2)}) async-start(bf16[8,2,256]{2,1,0:T(2,128)(2,1)} %reshape.49), calls=%async_computation.1 | async-start | bytes 16384 | tf_op jit(solution)/shard_map/all_to_all | solution.py:121
  765.3 1.8 fusion.17
  767.1 2.8 all-to-all-done.1
  769.9 0.6 reshape.50
  (8 shorter events, 0.0 us)
Async XLA Ops:
  7.2 497.5 %copy-start = (bf16[256,128]{1,0:T(8,128)(2,1)S(1)}, bf16[256,128]{1,0:T(8,128)(2,1)}, u32[]{:S(2)}) copy-start(bf16[256,128]{1,0:T(8,128)(2,1)} %param.10) | copy-start | bytes 196612
  7.2 336.5 %all-reduce.5.cloned.1.call-start = ((), (), s32[]{:S(2)}) async-start(), calls=%async_computation.4 | async-start | bytes 524288
  9.2 464.0 %all-gather.5.cloned.1.call-start = ((), (), s32[]{:S(2)}) async-start(), calls=%async_computation.3 | async-start | bytes 8404992 | tf_op jit(solution)/shard_map/all_gather | solution.py:110
  44.3 32.1 %copy-start.5 = (f32[1,32]{1,0:T(1,128)S(1)}, f32[1,32]{1,0:T(1,128)}, u32[]{:S(2)}) copy-start(f32[1,32]{1,0:T(1,128)} %param.9) | copy-start | bytes 388
  52.1 423.5 %all-to-all-start = ((bf16[512,2,2048]{2,1,0:T(2,128)(2,1)}), bf16[512,2,2048]{2,1,0:T(2,128)(2,1)}, u32[]{:S(2)}, u32[]{:S(2)}) async-start(bf16[512,2,2048]{2,1,0:T(2,128)(2,1)} %reshape.47), calls=%async_computation | async-start | bytes 8388608 | tf_op jit(solution)/shard_map/all_to_all | solution.py:102
  76.4 677.2 %reduce-scatter.4.cloned.1.call-start = ((), (), s32[]{:S(2)}) async-start(), calls=%async_computation.5 | async-start | bytes 1064960
  475.7 30.1 %copy-start.4 = (bf16[256,128]{1,0:T(8,128)(2,1)S(1)}, bf16[256,128]{1,0:T(8,128)(2,1)}, u32[]{:S(2)}) copy-start(bf16[256,128]{1,0:T(8,128)(2,1)} %param.11) | copy-start | bytes 196612
  506.0 1.2 copy-start.1
  506.5 0.7 copy-start.2
  507.0 0.7 copy-start.3
  755.5 14.4 %all-to-all-start.1 = ((bf16[8,2,256]{2,1,0:T(2,128)(2,1)}), bf16[8,2,256]{2,1,0:T(2,128)(2,1)S(1)}, u32[]{:S(2)}, u32[]{:S(2)}) async-start(bf16[8,2,256]{2,1,0:T(2,128)(2,1)} %reshape.49), calls=%async_computation.1 | async-start | bytes 16384 | tf_op jit(solution)/shard_map/all_to_all | solution.py:121
Sparse Core Ops, SparseCore 0:
  13.0 330.6 all-reduce.4
  348.1 125.1 all-gather.4
  514.5 238.9 reduce-scatter.3
